TPU v7x, 256 devices: a whole 4x4x8 slice. The times are simulated.
256 devices in a mesh: dp: 16 (over z, core), expert: 16 (over y, x).
Axes of the slice: x: 4, y: 4, z: 8, core: 2. Of those that a mesh axis runs over, the one named last changes fastest.
Arguments:
- cotangent: bfloat16 [32768, 2048], P(('dp', 'expert')), may hold values from -6 to 6
- saved_gate_up: bfloat16 [32768, 8, 1536], P(('dp', 'expert')), may hold values from -6 to 6
- route_ids: int32 [32768, 8], P(('dp', 'expert')), may hold values from 0 to 31, all different within a row; in each aligned block of 128 rows (0 to 127, 128 to 255, ...) at most 64 rows name the same one
- route_weights: float32 [32768, 8], P(('dp', 'expert')), may hold values from 0.05 to 1
- w_down: bfloat16 [32, 768, 2048], P('expert', 'dp'), may hold values from -0.21875 to 0.21875
Outputs:
- grad_gate_up: bfloat16 [32768, 8, 1536], P(('dp', 'expert'))
- route_grad: float32 [32768, 8], P(('dp', 'expert'))
- grad_down: float32 [32, 768, 2048], P('expert', 'dp')
Inputs may be any that keep to these rules, and one draw needn't show every extreme that they name: `route_ids`: within the rows of one device (aligned blocks of 128 tokens), no expert is named by more than 64 routes, and in every draw some expert is named by exactly 64; the 8 experts of a token are distinct.
All inputs are finite; a program needn't handle non-finite values.
Results may differ from a plain program's by a relative error of at most 0.02.
Values may be sent and summed in bfloat16 or wider, within the bound.
A program may use at most 128 MiB of HBM per device.

v0:
```python
import jax
import jax.numpy as jnp
from jax import lax
from jax.sharding import PartitionSpec as P


def slot_counts(ids, experts):
    routes = ids.shape[-1]
    onehot = (ids[..., None] == jnp.arange(experts, dtype=jnp.int32)).astype(jnp.bfloat16)
    lower = (jnp.arange(routes)[:, None] > jnp.arange(routes)[None, :]).astype(jnp.bfloat16)
    before = jnp.einsum("rq,...qe->...re", lower, onehot, preferred_element_type=jnp.float32)
    return jnp.sum(before * onehot.astype(jnp.float32), axis=-1).astype(jnp.int32)


def local(cotangent, saved_gate_up, route_ids, route_weights, w_down):
    tokens, top = route_ids.shape
    width = cotangent.shape[1]
    hidden_units = saved_gate_up.shape[2] // 2
    owners = lax.axis_size("expert")
    replicas = lax.axis_size("dp")
    me = lax.axis_index("expert")
    local_experts = w_down.shape[0]
    experts = local_experts * owners
    capacity = min(tokens, 2 * tokens * top // experts)
    routes = tokens * top
    cot_group = lax.all_gather(cotangent, "expert", axis=0, tiled=True)
    ids_group = lax.all_gather(route_ids.reshape(1, routes), "expert", axis=0, tiled=True)
    full_down = lax.all_gather(w_down, "dp", axis=1, tiled=True)
    gate = saved_gate_up[:, :, :hidden_units].astype(jnp.float32)
    up = saved_gate_up[:, :, hidden_units:].astype(jnp.float32)
    sig = jax.nn.sigmoid(gate)
    act = gate * sig
    hidden = (act * up).astype(jnp.bfloat16)
    weights = route_weights[:, :, None]
    scaled = (weights * hidden.astype(jnp.float32)).astype(jnp.bfloat16)
    flat_ids = route_ids.reshape(routes)
    slot = slot_counts(flat_ids, experts)
    position = flat_ids * capacity + slot
    slot_ids = jnp.arange(experts * capacity, dtype=jnp.int32)
    match = position[None, :] == slot_ids[:, None]
    route_of_slot = jnp.sum(
        jnp.where(match, jnp.arange(routes, dtype=jnp.int32)[None, :], 0), axis=1
    )
    filled = jnp.any(match, axis=1)
    h_rows = jnp.where(
        filled[:, None],
        scaled.reshape(routes, hidden_units)[route_of_slot],
        jnp.zeros((), jnp.bfloat16),
    )
    h_send = h_rows.reshape(owners, local_experts, capacity, hidden_units)
    slot_all = slot_counts(ids_group, experts)
    mine = me * local_experts + jnp.arange(local_experts, dtype=jnp.int32)
    pos_all = ids_group * capacity + slot_all
    want = (mine[:, None] * capacity + jnp.arange(capacity, dtype=jnp.int32)[None, :]).reshape(-1)
    hit = pos_all[:, None, :] == want[None, :, None]
    token_of = jnp.sum(
        jnp.where(hit, (jnp.arange(routes, dtype=jnp.int32) // top)[None, None, :], 0), axis=2
    )
    rows = (jnp.arange(owners, dtype=jnp.int32)[:, None] * tokens + token_of).reshape(
        owners, local_experts, capacity
    )
    rows = jnp.transpose(rows, (1, 0, 2)).reshape(local_experts, owners * capacity)
    h_recv = lax.all_to_all(h_send, "expert", split_axis=0, concat_axis=2, tiled=True)[0]
    h_recv, cot_group = lax.optimization_barrier((h_recv, cot_group))
    dy_recv = cot_group[rows]
    grads = jnp.einsum(
        "jsd,jfd->jsf", dy_recv, full_down, preferred_element_type=jnp.float32
    ).astype(jnp.bfloat16)
    back = lax.all_to_all(
        grads.reshape(1, local_experts, owners * capacity, hidden_units),
        "expert",
        split_axis=2,
        concat_axis=0,
        tiled=True,
    )
    parts = []
    for j in range(local_experts):
        part = jnp.einsum(
            "sf,sd->fd", h_recv[j], dy_recv[j], preferred_element_type=jnp.float32
        ).astype(jnp.bfloat16)
        parts.append(part.reshape(replicas, hidden_units // replicas, width))
    summed = lax.psum_scatter(jnp.stack(parts, axis=1), "dp", scatter_dimension=0, tiled=True)
    grad_down = summed[0].astype(jnp.float32)
    returned_rows = back.reshape(experts * capacity, hidden_units)[position]
    qf = returned_rows.reshape(tokens, top, hidden_units).astype(jnp.float32)
    route_grad = jnp.sum(qf * hidden.astype(jnp.float32), -1)
    d_hidden = weights * qf
    d_gate = d_hidden * up * sig * (1.0 + gate * (1.0 - sig))
    d_up = d_hidden * act
    grad_gate_up = jnp.concatenate([d_gate, d_up], -1).astype(jnp.bfloat16)
    return (grad_gate_up, route_grad, grad_down)


def solution(mesh):
    return jax.shard_map(
        local,
        mesh=mesh,
        in_specs=(
            P(("dp", "expert"), None),
            P(("dp", "expert"), None, None),
            P(("dp", "expert"), None),
            P(("dp", "expert"), None),
            P("expert", "dp", None),
        ),
        out_specs=(
            P(("dp", "expert"), None, None),
            P(("dp", "expert"), None),
            P("expert", "dp", None),
        ),
        check_vma=False,
    )
```

profile of v0, /device:TPU:1, one launch (start us, length us, event | category | flops | bytes accessed | tf_op | source)
XLA Modules:
  0.0 258.9 jit_solution(17816790262172470901)
XLA Ops:
  7.2 0.7 all-gather.4.cloned.1.call-update
  7.9 0.7 all-gather.6.cloned.1.call-update
  8.6 0.8 copy.43
  9.5 0.8 copy.42
  10.3 0.5 fusion.35
  10.9 1.0 fusion
  12.0 0.9 select_reduce_fusion.1
  12.9 3.4 %fusion.29 = (bf16[1024,768]{1,0:T(8,128)(2,1)S(1)}, bf16[128,8,768]{2,1,0:T(8,128)(2,1)}) fusion(f32[128,8]{1,0:T(8,128)S(1)} %copy.42, bf16[128,8,1536]{2,1,0:T(8,128)(2,1)} %param.6), kind=kLoop, calls=%fused_computation.45 | loop fusion | flops 8650752 | bytes 6295552 | tf_op jit(solution)/shard_map/reshape | solution.py:47
  16.3 9.4 %gather_fusion = bf16[2048,768]{1,0:T(8,128)(2,1)} fusion(bf16[1024,768]{1,0:T(8,128)(2,1)S(1)} %get-tuple-element.13, s32[2048]{0:T(1024)S(1)} %broadcast_clamp_fusion), kind=kCustom, calls=%fused_computation | custom fusion | bytes 6299648 | tf_op jit(solution)/shard_map/gather | solution.py:47
  25.7 3.5 %broadcast_select_fusion = bf16[16,2,64,768]{3,2,1,0:T(8,128)(2,1)} fusion(bf16[16,2,64,768]{3,2,1,0:T(8,128)(2,1)} %bitcast.64, pred[16,2,64]{2,1,0:T(4,128)(4,1)S(1)} %broadcast_in_dim.34), kind=kLoop, calls=%fused_computation.40 | loop fusion | flops 1572864 | bytes 6293504 | tf_op jit(solution)/shard_map/jit(_where)/select_n | solution.py:45
  29.2 7.5 %all-to-all-start = ((bf16[16,2,64,768]{3,2,1,0:T(8,128)(2,1)}), bf16[16,2,64,768]{3,2,1,0:T(8,128)(2,1)S(1)}, u32[]{:S(2)}, u32[]{:S(2)}) async-start(bf16[16,2,64,768]{3,2,1,0:T(8,128)(2,1)} %broadcast_select_fusion), calls=%async_computation | async-start | bytes 6291456 | tf_op jit(solution)/shard_map/all_to_all | solution.py:63
  36.9 69.4 %all-gather = s32[16,1,1024]{2,1,0:T(1,128)S(1)} all-gather(s32[1,1,1024]{2,1,0:T(1,128)S(1)} %reshape.207), channel_id=1, replica_groups=mesh['dp'=16,'expert'=16] {'expert'}, dimensions={0}, use_global_device_ids=true | all-gather | bytes 69632 | tf_op jit(solution)/shard_map/all_gather | solution.py:27
  106.4 1.4 fusion.27
  107.9 1.0 select_reduce_fusion
  109.2 1.9 copy.44
  111.0 6.2 %all-gather.4.cloned.1.call-done = bf16[2048,2048]{1,0:T(8,128)(2,1)} async-done(((bf16[128,2048]{1,0:T(8,128)(2,1)}), bf16[2048,2048]{1,0:T(8,128)(2,1)}) %all-gather.4.cloned.1.call-update) | async-done | bytes 8388624 | tf_op jit(solution)/shard_map/all_gather | solution.py:26
  117.3 21.1 %gather_fusion.1 = bf16[2048,2048]{1,0:T(8,128)(2,1)} fusion(bf16[2048,2048]{1,0:T(8,128)(2,1)} %all-gather.4.cloned.1.call-done, s32[2048]{0:T(1024)S(1)} %bitcast_clamp_fusion), kind=kCustom, calls=%fused_computation.1 | custom fusion | bytes 16785408 | tf_op jit(solution)/shard_map/gather | solution.py:65
  138.4 6.1 %fusion.10 = bf16[768,2048]{1,0:T(8,128)(2,1)S(1)} fusion(bf16[2048,2048]{1,0:T(8,128)(2,1)} %gather_fusion.1, bf16[2,1024,768]{2,1,0:T(8,128)(2,1)S(1)} %bitcast.66), kind=kOutput, calls=%fused_computation.25 | convolution fusion | flops 3222798336 | bytes 8912896 | tf_op jit(solution)/shard_map/sf,sd->fd/dot_general | solution.py:78
  144.5 3.7 %fusion.13 = bf16[768,2048]{1,0:T(8,128)(2,1)S(1)} fusion(bf16[2048,2048]{1,0:T(8,128)(2,1)S(1)} %copy-done.1, bf16[2,1024,768]{2,1,0:T(8,128)(2,1)S(1)} %bitcast.67), kind=kOutput, calls=%fused_computation.26 | convolution fusion | flops 3222798336 | bytes 8912896 | tf_op jit(solution)/shard_map/sf,sd->fd/dot_general | solution.py:78
  148.2 3.3 %pad_maximum_fusion = bf16[16,2,48,2048]{3,2,1,0:T(8,128)(2,1)} fusion(bf16[16,1,48,2048]{3,2,1,0:T(8,128)(2,1)S(1)} %bitcast.69, bf16[16,1,48,2048]{3,2,1,0:T(8,128)(2,1)S(1)} %bitcast.68), kind=kLoop, calls=%fused_computation.7 | loop fusion | flops 3145728 | bytes 12582912 | tf_op jit(solution)/shard_map/stack | solution.py:82
  151.5 12.3 %all-gather.6.cloned.1.call-done = bf16[2,768,2048]{2,1,0:T(8,128)(2,1)} async-done(((bf16[2,48,2048]{2,1,0:T(8,128)(2,1)}), bf16[2,768,2048]{2,1,0:T(8,128)(2,1)}) %all-gather.6.cloned.1.call-update) | async-done | bytes 6291472 | tf_op jit(solution)/shard_map/all_gather | solution.py:28
  163.8 11.0 %convert_bitcast_fusion = bf16[1,2,1024,768]{3,2,1,0:T(8,128)(2,1)S(1)} fusion(bf16[2,1024,2048]{2,1,0:T(8,128)(2,1)} %bitcast.65, bf16[2,768,2048]{2,1,0:T(8,128)(2,1)} %all-gather.6.cloned.1.call-done), kind=kOutput, calls=%fused_computation.39 | convolution fusion | flops 6444023808 | bytes 17825792 | tf_op jit(solution)/shard_map/jsd,jfd->jsf/dot_general | solution.py:66
  174.8 4.9 %copy.47 = bf16[1,2,1024,768]{3,1,0,2:T(2,128)(2,1)} copy(bf16[1,2,1024,768]{3,2,1,0:T(8,128)(2,1)S(1)} %convert_bitcast_fusion) | data formatting | bytes 6291456 | tf_op jit(solution)/shard_map/reshape | solution.py:70
  179.7 6.7 %all-to-all-start.1 = ((bf16[1,2,1024,768]{3,1,0,2:T(2,128)(2,1)}), bf16[1,2,1024,768]{3,1,0,2:T(2,128)(2,1)S(1)}, u32[]{:S(2)}, u32[]{:S(2)}) async-start(bf16[1,2,1024,768]{3,1,0,2:T(2,128)(2,1)} %copy.47), calls=%async_computation.1 | async-start | bytes 6291456 | tf_op jit(solution)/shard_map/all_to_all | solution.py:69
  186.6 47.5 %all-to-all-done.1 = bf16[1,2,1024,768]{3,1,0,2:T(2,128)(2,1)S(1)} async-done(((bf16[1,2,1024,768]{3,1,0,2:T(2,128)(2,1)}), bf16[1,2,1024,768]{3,1,0,2:T(2,128)(2,1)S(1)}, u32[]{:S(2)}, u32[]{:S(2)}) %all-to-all-start.1) | async-done | bytes 3145760 | tf_op jit(solution)/shard_map/all_to_all | solution.py:69
  234.2 1.7 copy-done
  235.9 2.5 copy.48
  238.4 5.2 %gather_fusion.2 = bf16[1024,768]{1,0:T(8,128)(2,1)} fusion(bf16[2048,768]{1,0:T(8,128)(2,1)S(1)} %bitcast.62, s32[1024]{0:T(1024)S(1)} %broadcast_clamp_fusion.1), kind=kCustom, calls=%fused_computation.2 | custom fusion | bytes 3149824 | tf_op jit(solution)/shard_map/gather | solution.py:84
  243.6 4.2 %fusion.20 = (bf16[128,8,768]{2,1,0:T(8,128)(2,1)S(1)}, bf16[128,8,768]{2,1,0:T(8,128)(2,1)S(1)}, f32[128,8]{1,0:T(8,128)S(1)}) fusion(bf16[1024,768]{1,0:T(8,128)(2,1)} %gather_fusion.2, f32[128,8]{1,0:T(8,128)S(1)} %copy.42, bf16[128,8,1536]{2,1,0:T(8,128)(2,1)} %param.6, bf16[128,8,768]{2,1,0:T(8,128)(2,1)} %get-tuple-element.14), kind=kLoop, calls=%fused_computation.31 | loop fusion | flops 15727616 | bytes 9445376 | tf_op jit(solution)/shard_map/convert.2
  247.8 0.7 copy.52
  248.5 1.9 pad_maximum_fusion.1
  250.4 1.9 bitcast_convert_fusion
  (38 shorter events, 1.1 us)
Async XLA Ops:
  7.2 110.1 %all-gather.4.cloned.1.call-start = ((), (), s32[]{:S(2)}) async-start(), calls=%async_computation.3 | async-start | bytes 8912896 | tf_op jit(solution)/shard_map/all_gather | solution.py:26
  7.9 155.9 %all-gather.6.cloned.1.call-start = ((), (), s32[]{:S(2)}) async-start(), calls=%async_computation.4 | async-start | bytes 6684672 | tf_op jit(solution)/shard_map/all_gather | solution.py:28
  29.2 80.0 %all-to-all-start = ((bf16[16,2,64,768]{3,2,1,0:T(8,128)(2,1)}), bf16[16,2,64,768]{3,2,1,0:T(8,128)(2,1)S(1)}, u32[]{:S(2)}, u32[]{:S(2)}) async-start(bf16[16,2,64,768]{3,2,1,0:T(8,128)(2,1)} %broadcast_select_fusion), calls=%async_computation | async-start | bytes 6291456 | tf_op jit(solution)/shard_map/all_to_all | solution.py:63
  36.7 213.7 %reduce-scatter.2.cloned.1.call-start = ((), (), s32[]{:S(2)}) async-start(), calls=%async_computation.5 | async-start | bytes 6684672 | tf_op jit(solution)/shard_map/reduce_scatter | solution.py:82
  117.3 21.1 %copy-start.2 = (bf16[16,2,64,768]{3,2,0,1:T(8,128)(2,1)S(1)}, bf16[16,2,64,768]{3,2,0,1:T(8,128)(2,1)}, u32[]{:S(2)}) copy-start(bf16[16,2,64,768]{3,2,0,1:T(8,128)(2,1)} %copy.44) | copy-start | bytes 9437188
  138.4 6.1 %copy-start.1 = (bf16[2048,2048]{1,0:T(8,128)(2,1)S(1)}, bf16[2048,2048]{1,0:T(8,128)(2,1)}, u32[]{:S(2)}) copy-start(bf16[2048,2048]{1,0:T(8,128)(2,1)} %gather_fusion.1) | copy-start | bytes 25165828
  179.7 6.7 %copy-start.3 = (s32[128,8]{0,1:T(8,128)S(1)}, s32[128,8]{0,1:T(8,128)}, u32[]{:S(2)}) copy-start(s32[128,8]{0,1:T(8,128)} %param.7) | copy-start | bytes 12292
  179.7 54.5 %all-to-all-start.1 = ((bf16[1,2,1024,768]{3,1,0,2:T(2,128)(2,1)}), bf16[1,2,1024,768]{3,1,0,2:T(2,128)(2,1)S(1)}, u32[]{:S(2)}, u32[]{:S(2)}) async-start(bf16[1,2,1024,768]{3,1,0,2:T(2,128)(2,1)} %copy.47), calls=%async_computation.1 | async-start | bytes 6291456 | tf_op jit(solution)/shard_map/all_to_all | solution.py:69
  234.2 1.7 copy-start
Sparse Core Ops, SparseCore 0:
  10.4 106.7 all-gather.3
  119.1 44.6 all-gather.5
  166.4 62.4 reduce-scatter.1
where the time goes:
time: 259 us
  blocking collectives  69.4 us (27%)
  waiting for transfers between devices  67.4 us (26%)
  local copies, waits for them, and re-layouts  49.7 us (19%)
  matrix products  22.8 us (9%)
  other arithmetic  21.4 us (8%)
  starting transfers between devices  14.3 us (6%)
  between operations  14 us (5%)
    all_gather x1, blocking collectives, local(): lax.all_gather(route_ids.reshape(1, routes), 'expert', axis=0, tiled=True)  69.4 us
    all_to_all x1, waiting for transfers between devices, local(): lax.all_to_all(grads.reshape(1, local_experts, owners * capacity, hidden_...  47.5 us
    gather x1, local copies, waits for them, and re-layouts, local(): dy_recv = cot_group[rows]  21.1 us
    all_gather x1, waiting for transfers between devices, local(): full_down = lax.all_gather(w_down, 'dp', axis=1, tiled=True)  12.3 us
    dot_general x1, matrix products, local(): jnp.einsum('jsd,jfd->jsf', dy_recv, full_down, preferred_element_type=jnp...  11 us
    dot_general x2, matrix products, local(): jnp.einsum('sf,sd->fd', h_recv[j], dy_recv[j], preferred_element_type=jnp...  9.8 us
    gather x1, local copies, waits for them, and re-layouts, local(): scaled.reshape(routes, hidden_units)[route_of_slot]  9.4 us
    all_to_all x1, starting transfers between devices, local(): lax.all_to_all(h_send, 'expert', split_axis=0, concat_axis=2, tiled=True)[0]  7.51 us
  transfers between devices with their start and end apart: 5, of which 3 were waited for; matrix products, arithmetic and copies ran while one was open for 35% of the time, Pallas kernels for 0%

commit v1 on v0

--- a/solution.py
+++ b/solution.py
@@ -25,7 +25,13 @@
     routes = tokens * top
     cot_group = lax.all_gather(cotangent, "expert", axis=0, tiled=True)
     ids_group = lax.all_gather(route_ids.reshape(1, routes), "expert", axis=0, tiled=True)
-    full_down = lax.all_gather(w_down, "dp", axis=1, tiled=True)
+    create_members_all_by_axis = lambda obj, axis_tag, where_dim: jnp.concatenate(
+        lax.all_to_all(
+            jnp.stack([obj for _ in range(lax.psum(1, axis_tag))], axis=0), axis_tag, 0, 0
+        ),
+        axis=where_dim,
+    )
+    full_down = create_members_all_by_axis(w_down, "dp", 1)
     gate = saved_gate_up[:, :, :hidden_units].astype(jnp.float32)
     up = saved_gate_up[:, :, hidden_units:].astype(jnp.float32)
     sig = jax.nn.sigmoid(gate)

time: 259 us -> 336 us (1.30)
  waiting for transfers between devices: 67.4 us -> 143 us
  local copies, waits for them, and re-layouts: 49.7 us -> 56.6 us
    all_to_all x1, waiting for transfers between devices: 0.01 us -> 93.8 us  [local(): lax.all_to_all(jnp.stack([obj for _ in range(lax.psum(1, axis_tag))], axi...]
    all_gather x1, blocking collectives: 69.4 us -> 18.9 us  [local(): lax.all_gather(route_ids.reshape(1, routes), 'expert', axis=0, tiled=True)]
    all_to_all x0 -> x1, blocking collectives: none -> 48.9 us  [local(): lax.all_to_all(h_send, 'expert', split_axis=0, concat_axis=2, tiled=True)[0]]
    all_gather x1 -> x0, waiting for transfers between devices: 12.3 us -> none  [local(): full_down = lax.all_gather(w_down, 'dp', axis=1, tiled=True)]
    all_gather x1, waiting for transfers between devices: 6.22 us -> 0.01 us  [local(): cot_group = lax.all_gather(cotangent, 'expert', axis=0, tiled=True)]
    reshape x0 -> x1, local copies, waits for them, and re-layouts: none -> 3.48 us  [local(): jnp.concatenate(lax.all_to_all(jnp.stack([obj for _ in range(lax.psum(1,...]
    another operation x0 -> x1, local copies, waits for them, and re-layouts: none -> 3.45 us  [local(): jnp.stack([obj for _ in range(lax.psum(1, axis_tag))], axis=0)]
  transfers between devices with their start and end apart: 5 -> 4, of which waited for: 3 -> 2; matrix products, arithmetic and copies ran while one was open for 35% -> 28% of each run, Pallas kernels for 0% -> 0%
where the time goes in v1:
time: 336 us
  waiting for transfers between devices  143 us (43%)
  blocking collectives  67.8 us (20%)
  local copies, waits for them, and re-layouts  56.6 us (17%)
  matrix products  20.9 us (6%)
  other arithmetic  20.2 us (6%)
  between operations  14.3 us (4%)
  starting transfers between devices  12.9 us (4%)
    all_to_all x1, waiting for transfers between devices, local(): lax.all_to_all(jnp.stack([obj for _ in range(lax.psum(1, axis_tag))], axi...  93.8 us
    all_to_all x1, blocking collectives, local(): lax.all_to_all(h_send, 'expert', split_axis=0, concat_axis=2, tiled=True)[0]  48.9 us
    all_to_all x1, waiting for transfers between devices, local(): lax.all_to_all(grads.reshape(1, local_experts, owners * capacity, hidden_...  48.9 us
    gather x1, local copies, waits for them, and re-layouts, local(): dy_recv = cot_group[rows]  21.1 us
    all_gather x1, blocking collectives, local(): lax.all_gather(route_ids.reshape(1, routes), 'expert', axis=0, tiled=True)  18.9 us
    dot_general x2, matrix products, local(): jnp.einsum('sf,sd->fd', h_recv[j], dy_recv[j], preferred_element_type=jnp...  9.73 us
    gather x1, local copies, waits for them, and re-layouts, local(): scaled.reshape(routes, hidden_units)[route_of_slot]  9.4 us
    dot_general x1, matrix products, local(): jnp.einsum('jsd,jfd->jsf', dy_recv, full_down, preferred_element_type=jnp...  9.19 us
  transfers between devices with their start and end apart: 4, of which 2 were waited for; matrix products, arithmetic and copies ran while one was open for 28% of the time, Pallas kernels for 0%

profile of v1, /device:TPU:1, one launch (start us, length us, event | category | flops | bytes accessed | tf_op | source)
XLA Modules:
  0.0 336.0 jit_solution(13003331292949876427)
XLA Ops:
  7.2 0.7 all-gather.3.cloned.1.call-update
  7.9 0.8 copy.43
  8.7 0.8 copy.44
  10.1 1.0 fusion
  11.2 0.9 select_reduce_fusion.1
  12.2 3.4 %fusion.29 = (bf16[1024,768]{1,0:T(8,128)(2,1)S(1)}, bf16[128,8,768]{2,1,0:T(8,128)(2,1)}) fusion(f32[128,8]{1,0:T(8,128)S(1)} %copy.43, bf16[128,8,1536]{2,1,0:T(8,128)(2,1)} %param.6), kind=kLoop, calls=%fused_computation.45 | loop fusion | flops 8650752 | bytes 6295552 | tf_op jit(solution)/shard_map/reshape | solution.py:53
  15.6 9.4 %gather_fusion = bf16[2048,768]{1,0:T(8,128)(2,1)} fusion(bf16[1024,768]{1,0:T(8,128)(2,1)S(1)} %get-tuple-element.13, s32[2048]{0:T(1024)S(1)} %broadcast_clamp_fusion), kind=kCustom, calls=%fused_computation | custom fusion | bytes 6299648 | tf_op jit(solution)/shard_map/gather | solution.py:53
  25.0 2.3 broadcast_select_fusion
  27.2 48.9 %all_to_all.35 = bf16[16,2,64,768]{3,2,1,0:T(8,128)(2,1)S(1)} all-to-all(bf16[16,2,64,768]{3,2,1,0:T(8,128)(2,1)S(1)} %broadcast_select_fusion), channel_id=1, replica_groups=mesh['dp'=16,'expert'=16] {'expert'}, dimensions={0} | all-to-all | bytes 6291456 | tf_op jit(solution)/shard_map/all_to_all | solution.py:69
  76.2 3.4 %stack.4 = bf16[16,2,48,2048]{3,2,1,0:T(8,128)(2,1)} broadcast(bf16[2,48,2048]{2,1,0:T(8,128)(2,1)S(1)} %copy-done.3), dimensions={1,2,3} | broadcast | bytes 6684672 | tf_op jit(solution)/shard_map/stack | solution.py:30
  79.6 8.8 %all-to-all-start.1 = ((bf16[16,2,48,2048]{3,2,1,0:T(8,128)(2,1)}), bf16[16,2,48,2048]{3,2,1,0:T(8,128)(2,1)}, u32[]{:S(2)}, u32[]{:S(2)}) async-start(bf16[16,2,48,2048]{3,2,1,0:T(8,128)(2,1)} %stack.4), calls=%async_computation.1 | async-start | bytes 12582912 | tf_op jit(solution)/shard_map/all_to_all | solution.py:29
  88.7 18.9 %all-gather = s32[16,1,1024]{2,1,0:T(1,128)S(1)} all-gather(s32[1,1,1024]{2,1,0:T(1,128)S(1)} %reshape.217), channel_id=1, replica_groups=mesh['dp'=16,'expert'=16] {'expert'}, dimensions={0}, use_global_device_ids=true | all-gather | bytes 69632 | tf_op jit(solution)/shard_map/all_gather | solution.py:27
  107.6 1.4 fusion.27
  109.1 1.0 select_reduce_fusion
  110.3 1.9 copy.45
  112.2 21.1 %gather_fusion.1 = bf16[2048,2048]{1,0:T(8,128)(2,1)} fusion(bf16[2048,2048]{1,0:T(8,128)(2,1)} %all-gather.3.cloned.1.call-done, s32[2048]{0:T(1024)S(1)} %bitcast_clamp_fusion), kind=kCustom, calls=%fused_computation.1 | custom fusion | bytes 16785408 | tf_op jit(solution)/shard_map/gather | solution.py:71
  133.3 6.0 %fusion.13 = bf16[768,2048]{1,0:T(8,128)(2,1)S(1)} fusion(bf16[2048,2048]{1,0:T(8,128)(2,1)} %gather_fusion.1, bf16[2,1024,768]{2,1,0:T(8,128)(2,1)S(1)} %bitcast.69), kind=kOutput, calls=%fused_computation.26 | convolution fusion | flops 3222798336 | bytes 8912896 | tf_op jit(solution)/shard_map/sf,sd->fd/dot_general | solution.py:84
  139.4 3.7 %fusion.10 = bf16[768,2048]{1,0:T(8,128)(2,1)S(1)} fusion(bf16[2048,2048]{1,0:T(8,128)(2,1)S(1)} %copy-done.1, bf16[2,1024,768]{2,1,0:T(8,128)(2,1)S(1)} %bitcast.70), kind=kOutput, calls=%fused_computation.25 | convolution fusion | flops 3222798336 | bytes 8912896 | tf_op jit(solution)/shard_map/sf,sd->fd/dot_general | solution.py:84
  143.1 3.3 pad_maximum_fusion
  146.4 93.8 %all-to-all-done.1 = bf16[16,2,48,2048]{3,2,1,0:T(8,128)(2,1)} async-done(((bf16[16,2,48,2048]{3,2,1,0:T(8,128)(2,1)}), bf16[16,2,48,2048]{3,2,1,0:T(8,128)(2,1)}, u32[]{:S(2)}, u32[]{:S(2)}) %all-to-all-start.1) | async-done | bytes 6291488 | tf_op jit(solution)/shard_map/all_to_all | solution.py:29
  240.2 3.5 %copy.48 = bf16[2,16,48,2048]{3,2,1,0:T(8,128)(2,1)S(1)} copy(bf16[2,16,48,2048]{3,2,0,1:T(8,128)(2,1)} %bitcast.11) | data formatting | bytes 12582912 | tf_op jit(solution)/shard_map/reshape | solution.py:28
  243.6 9.2 %convert_bitcast_fusion = bf16[1,2,1024,768]{3,2,1,0:T(8,128)(2,1)S(1)} fusion(bf16[2,1024,2048]{2,1,0:T(8,128)(2,1)} %bitcast.67, bf16[2,768,2048]{2,1,0:T(8,128)(2,1)S(1)} %bitcast.68), kind=kOutput, calls=%fused_computation.39 | convolution fusion | flops 6444023808 | bytes 17825792 | tf_op jit(solution)/shard_map/jsd,jfd->jsf/dot_general | solution.py:72
  252.8 4.9 %copy.49 = bf16[1,2,1024,768]{3,1,0,2:T(2,128)(2,1)} copy(bf16[1,2,1024,768]{3,2,1,0:T(8,128)(2,1)S(1)} %convert_bitcast_fusion) | data formatting | bytes 6291456 | tf_op jit(solution)/shard_map/reshape | solution.py:76
  257.7 4.1 %all-to-all-start.2 = ((bf16[1,2,1024,768]{3,1,0,2:T(2,128)(2,1)}), bf16[1,2,1024,768]{3,1,0,2:T(2,128)(2,1)S(1)}, u32[]{:S(2)}, u32[]{:S(2)}) async-start(bf16[1,2,1024,768]{3,1,0,2:T(2,128)(2,1)} %copy.49), calls=%async_computation.2 | async-start | bytes 6291456 | tf_op jit(solution)/shard_map/all_to_all | solution.py:75
  262.1 48.9 %all-to-all-done.2 = bf16[1,2,1024,768]{3,1,0,2:T(2,128)(2,1)S(1)} async-done(((bf16[1,2,1024,768]{3,1,0,2:T(2,128)(2,1)}), bf16[1,2,1024,768]{3,1,0,2:T(2,128)(2,1)S(1)}, u32[]{:S(2)}, u32[]{:S(2)}) %all-to-all-start.2) | async-done | bytes 3145760 | tf_op jit(solution)/shard_map/all_to_all | solution.py:75
  311.0 1.7 copy-done
  312.6 2.5 copy.50
  315.2 5.2 %gather_fusion.2 = bf16[1024,768]{1,0:T(8,128)(2,1)} fusion(bf16[2048,768]{1,0:T(8,128)(2,1)S(1)} %bitcast.64, s32[1024]{0:T(1024)S(1)} %broadcast_clamp_fusion.1), kind=kCustom, calls=%fused_computation.2 | custom fusion | bytes 3149824 | tf_op jit(solution)/shard_map/gather | solution.py:90
  320.4 4.2 %fusion.20 = (bf16[128,8,768]{2,1,0:T(8,128)(2,1)S(1)}, bf16[128,8,768]{2,1,0:T(8,128)(2,1)S(1)}, f32[128,8]{1,0:T(8,128)S(1)}) fusion(bf16[1024,768]{1,0:T(8,128)(2,1)} %gather_fusion.2, f32[128,8]{1,0:T(8,128)S(1)} %copy.43, bf16[128,8,1536]{2,1,0:T(8,128)(2,1)} %param.6, bf16[128,8,768]{2,1,0:T(8,128)(2,1)} %get-tuple-element.14), kind=kLoop, calls=%fused_computation.31 | loop fusion | flops 15727616 | bytes 9445376 | tf_op jit(solution)/shard_map/convert.2
  324.6 0.7 copy.54
  325.3 1.9 pad_maximum_fusion.1
  327.2 1.9 bitcast_convert_fusion
  (40 shorter events, 1.6 us)
Async XLA Ops:
  7.2 105.0 %all-gather.3.cloned.1.call-start = ((), (), s32[]{:S(2)}) async-start(), calls=%async_computation.4 | async-start | bytes 8912896 | tf_op jit(solution)/shard_map/all_gather | solution.py:26
  27.2 48.9 %copy-start.3 = (bf16[2,48,2048]{2,1,0:T(8,128)(2,1)S(1)}, bf16[2,48,2048]{2,1,0:T(8,128)(2,1)}, u32[]{:S(2)}) copy-start(bf16[2,48,2048]{2,1,0:T(8,128)(2,1)} %param.9) | copy-start | bytes 1179652
  79.6 160.5 %all-to-all-start.1 = ((bf16[16,2,48,2048]{3,2,1,0:T(8,128)(2,1)}), bf16[16,2,48,2048]{3,2,1,0:T(8,128)(2,1)}, u32[]{:S(2)}, u32[]{:S(2)}) async-start(bf16[16,2,48,2048]{3,2,1,0:T(8,128)(2,1)} %stack.4), calls=%async_computation.1 | async-start | bytes 12582912 | tf_op jit(solution)/shard_map/all_to_all | solution.py:29
  88.4 238.8 %reduce-scatter.2.cloned.1.call-start = ((), (), s32[]{:S(2)}) async-start(), calls=%async_computation.5 | async-start | bytes 6684672 | tf_op jit(solution)/shard_map/reduce_scatter | solution.py:88
  112.2 21.1 %copy-start.2 = (bf16[16,2,64,768]{3,2,0,1:T(8,128)(2,1)S(1)}, bf16[16,2,64,768]{3,2,0,1:T(8,128)(2,1)}, u32[]{:S(2)}) copy-start(bf16[16,2,64,768]{3,2,0,1:T(8,128)(2,1)} %copy.45) | copy-start | bytes 9437188
  133.3 6.0 %copy-start.1 = (bf16[2048,2048]{1,0:T(8,128)(2,1)S(1)}, bf16[2048,2048]{1,0:T(8,128)(2,1)}, u32[]{:S(2)}) copy-start(bf16[2048,2048]{1,0:T(8,128)(2,1)} %gather_fusion.1) | copy-start | bytes 25165828
  257.7 4.1 %copy-start.4 = (s32[128,8]{0,1:T(8,128)S(1)}, s32[128,8]{0,1:T(8,128)}, u32[]{:S(2)}) copy-start(s32[128,8]{0,1:T(8,128)} %param.7) | copy-start | bytes 12292
  257.7 53.2 %all-to-all-start.2 = ((bf16[1,2,1024,768]{3,1,0,2:T(2,128)(2,1)}), bf16[1,2,1024,768]{3,1,0,2:T(2,128)(2,1)S(1)}, u32[]{:S(2)}, u32[]{:S(2)}) async-start(bf16[1,2,1024,768]{3,1,0,2:T(2,128)(2,1)} %copy.49), calls=%async_computation.2 | async-start | bytes 6291456 | tf_op jit(solution)/shard_map/all_to_all | solution.py:75
  311.0 1.7 copy-start
Sparse Core Ops, SparseCore 0:
  10.4 100.7 all-gather.2
  146.5 123.6 reduce-scatter.1
